TPU v7x, 32 devices: a whole 2x2x4 slice. The times are simulated.
32 devices in a mesh: group: 2 (over y), row: 4 (over z), col: 2 (over x), sub: 2 (over core).
Axes of the slice: x: 2, y: 2, z: 4, core: 2. Of those that a mesh axis runs over, the one named last changes fastest.
Arguments:
- anomalies: bfloat16 [2048, 2048], P(('group', 'row', 'sub')), parts along dimension 0, may hold values from -6 to 6
- innovations: float32 [4096], P(('group', 'row', 'col', 'sub')), parts along dimension 0, may hold values from -12 to 12
- obs_error: float32 [4096], P(('group', 'row', 'col', 'sub')), parts along dimension 0, may hold values from 0.5 to 2
- track_pos: float32 [4096], P('group'), parts along dimension 0, may hold values from 0 to 1
- taper_class: int32 [8, 4], P('group'), parts along dimension 0, may hold values from 0 to 3, as said below
Outputs:
- solution: float32 [4096], P(('group', 'row', 'col', 'sub')), parts along dimension 0
- residual: float32 [4096], P(('group', 'row', 'col', 'sub')), parts along dimension 0
There are 2 independent parts, one for each index of `group`. A program takes and returns all parts, laid end to end along the dimension named above; each array names one. Nothing has to cross between parts.
Inputs may be any that keep to these rules, and one draw needn't show every extreme that they name: `taper_class`: tiles are spatial blocks of the region, laid along the plume in an order given by a permutation pos of the 4 tiles; entry (a, b) is the distance |pos[a] - pos[b]| in tiles.
All inputs are finite; a program needn't handle non-finite values.
Results may differ from a plain program's by a relative error of at most 0.0003.
Values may be sent and summed in bfloat16 or wider, within the bound.
No kernel may reach another device: no remote copies, remote signals or barrier semaphores. Data moves between devices by JAX's collectives and lax.ppermute only.
A program may use at most 64 MiB of HBM per device.

v0:
```python
import jax
import jax.numpy as jnp
from jax import lax
from jax.sharding import PartitionSpec as P

ITERS = 2
track_width = 0.0001


def squares(residual):
    return lax.psum(jnp.sum(residual * residual), ("row", "col", "sub"))


def per_device(anomalies, innovations, obs_error, track_pos, taper_class):
    row_count = lax.axis_size("row")
    col_count = lax.axis_size("col")
    sub_count = lax.axis_size("sub")
    row_index = lax.axis_index("row")
    col_index = lax.axis_index("col")
    local_members, total_obs = anomalies.shape
    block_len = total_obs // row_count
    quarter_len = block_len // col_count
    member_total = local_members * row_count * sub_count
    inverse_members = 1.0 / (member_total - 1)
    reach_tiles = max(2, row_count // 4)
    class_row = lax.dynamic_index_in_dim(taper_class, row_index, 0, keepdims=False)
    tile_weight = jnp.maximum(0.0, 1.0 - class_row.astype(jnp.float32) / reach_tiles)
    row_pos = lax.dynamic_slice_in_dim(track_pos, row_index * block_len, block_len, 0)
    col_pos = lax.dynamic_index_in_dim(
        track_pos.reshape(row_count, col_count, quarter_len), col_index, 1, keepdims=False
    )
    own_block = lax.all_to_all(anomalies, "row", split_axis=1, concat_axis=0, tiled=True)
    own_quarter = lax.dynamic_slice_in_dim(own_block, col_index * quarter_len, quarter_len, 1)

    def one_tile(piece, block_index, keep_factor):
        product = jnp.einsum("mi,mq->iq", own_block, piece, preferred_element_type=jnp.float32)
        column_pos = lax.dynamic_index_in_dim(col_pos, block_index, 0, keepdims=False)
        weight_here = lax.dynamic_index_in_dim(tile_weight, block_index, 0, keepdims=False)
        distance = row_pos[:, None] - column_pos[None, :]
        taper = weight_here * keep_factor * jnp.exp(-(distance * distance) / track_width)
        return product * (taper * inverse_members)

    def one_entry(entry):
        return one_tile(entry[0], entry[1], 1.0)

    piece = lax.all_gather(own_quarter[None], "row", axis=0, tiled=True)
    indices = jnp.arange(piece.shape[0], dtype=jnp.int32)
    tiles = lax.map(one_entry, (piece, indices))
    solution = jnp.zeros_like(innovations)
    residual = innovations
    direction_vec = innovations
    norm_now = squares(residual)
    for turn_index in range(ITERS):
        column_vec = lax.all_gather(direction_vec, ("row", "sub"), axis=0, tiled=True).reshape(
            row_count, quarter_len
        )
        direct = jnp.einsum("jiq,jq->i", tiles, column_vec, precision=lax.Precision.HIGHEST)
        extra = obs_error * direction_vec
        own_part = lax.psum_scatter(direct, ("col", "sub"), scatter_dimension=0, tiled=True)
        image = own_part + extra
        alpha = norm_now / lax.psum(jnp.sum(direction_vec * image), ("row", "col", "sub"))
        solution = solution + alpha * direction_vec
        residual = residual - alpha * image
        if turn_index + 1 < ITERS:
            norm_next = squares(residual)
            direction_vec = residual + norm_next / norm_now * direction_vec
            norm_now = norm_next
    return (solution, residual)


def solution(mesh):
    in_specs = (
        P(("group", "row", "sub"), None),
        P(("group", "row", "col", "sub")),
        P(("group", "row", "col", "sub")),
        P("group"),
        P("group", None),
    )
    out_specs = (P(("group", "row", "col", "sub")), P(("group", "row", "col", "sub")))
    return jax.shard_map(
        per_device, mesh=mesh, in_specs=in_specs, out_specs=out_specs, check_vma=False
    )
```

profile of v0, /device:TPU:0, one launch (start us, length us, event | category | flops | bytes accessed | tf_op | source)
XLA Modules:
  0.0 207.6 jit_solution(16276653144272945120)
XLA Ops:
  7.2 0.0 copy-start.3
  7.2 0.0 copy-start
  7.2 0.0 copy-start.1
  7.2 1.9 copy.16
  9.1 6.3 %all-to-all-start = ((bf16[128,4,512]{2,0,1:T(8,128)(2,1)}), bf16[128,4,512]{2,0,1:T(8,128)(2,1)S(1)}, u32[]{:S(2)}, u32[]{:S(2)}) async-start(bf16[128,4,512]{2,0,1:T(8,128)(2,1)} %bitcast.41), calls=%async_computation | async-start | bytes 1048576 | tf_op jit(solution)/shard_map/all_to_all | solution.py:32
  15.4 0.0 all-gather.5.cloned.1.call-start
  15.4 14.5 %all-to-all-done = bf16[128,4,512]{2,0,1:T(8,128)(2,1)S(1)} async-done(((bf16[128,4,512]{2,0,1:T(8,128)(2,1)}), bf16[128,4,512]{2,0,1:T(8,128)(2,1)S(1)}, u32[]{:S(2)}, u32[]{:S(2)}) %all-to-all-start) | async-done | bytes 524320 | tf_op jit(solution)/shard_map/all_to_all | solution.py:32
  29.9 0.7 constant_dynamic-slice_fusion.3
  30.6 0.0 all-gather.5.cloned.1.call-update
  30.7 0.0 copy-done
  30.7 0.1 dynamic_slice.32
  30.8 0.0 copy-done.3
  30.8 0.6 dynamic-slice
  32.0 0.0 copy-done.1
  32.1 9.8 %all-gather.1 = f32[8,1,128]{2,1,0:T(1,128)S(1)} all-gather(f32[1,1,128]{2,1,0:T(1,128)S(1)} %bitcast.64), channel_id=1, replica_groups=mesh['group'=2,'row'=4,'col'=2,'sub'=2] {'row','sub'}, dimensions={0}, use_global_device_ids=true | all-gather | bytes 4608 | tf_op jit(solution)/shard_map/all_gather | solution.py:54
  41.8 0.7 maximum_bitcast_fusion
  42.5 15.3 %all-gather.5.cloned.1.call-done = bf16[2048,256]{1,0:T(8,128)(2,1)} async-done(((bf16[512,256]{1,0:T(8,128)(2,1)}), bf16[2048,256]{1,0:T(8,128)(2,1)}) %all-gather.5.cloned.1.call-update) | async-done | bytes 1048592 | tf_op jit(solution)/shard_map/all_gather | solution.py:46
  57.8 20.4 %while.10 = (s32[]{:T(128)}, f32[4,512,256]{1,2,0:T(8,128)S(1)}, bf16[4,512,256]{2,1,0:T(8,128)(2,1)}, bf16[512,512]{1,0:T(8,128)(2,1)S(1)}, s32[4]{0:T(128)S(1)...) while((s32[]{:T(128)}, f32[4,512,256]{1,2,0:T(8,128)S(1)}, ...), condition=%wide.region_3.4_spmd, body=%wide.region_2.3_spmd.sunk | while | flops 135135232 | bytes 1317547 | solution.py:48
  57.8 0.6 dynamic_slice.56
  60.4 0.6 dynamic_slice.57
  61.0 1.9 fusion.21
  62.9 0.6 dynamic_slice.56
  65.5 0.6 dynamic_slice.57
  66.1 1.9 fusion.21
  68.0 0.6 dynamic_slice.56
  70.6 0.6 dynamic_slice.57
  71.2 1.9 fusion.21
  73.1 0.6 dynamic_slice.56
  75.7 0.6 dynamic_slice.57
  76.3 1.9 fusion.21
  78.2 0.0 copy-start.2
  78.2 1.2 fusion.9
  79.4 6.4 %all-reduce = f32[512]{0:T(512)S(1)} all-reduce(f32[512]{0:T(512)S(1)} %bitcast.66), channel_id=3, replica_groups=mesh['group'=2,'row'=4,'col'=2,'sub'=2] {'col','sub'}, use_global_device_ids=true, to_apply=%region_4.5.clone | all-reduce | flops 512 | bytes 4096
  85.8 0.0 copy-done.2
  85.8 0.7 multiply_reduce_fusion.2
  86.5 31.6 %all-reduce.2 = (f32[]{:T(128)}, f32[]{:T(128)}) all-reduce(f32[]{:T(128)} %get-tuple-element.46, f32[]{:T(128)} %get-tuple-element.45), channel_id=1, replica_groups=mesh['group'=2,'row'=4,'col'=2,'sub'=2] {'row','col','sub'}, use_global_device_ids=true, to_apply=%region_1.2 | all-reduce | flops 2 | bytes 16 | tf_op jit(solution)/shard_map/psum | solution.py:11
  119.5 0.7 multiply_reduce_fusion.1
  120.1 30.1 %psum.30 = f32[]{:T(128)} all-reduce(f32[]{:T(128)} %get-tuple-element.65), channel_id=1, replica_groups=mesh['group'=2,'row'=4,'col'=2,'sub'=2] {'row','col','sub'}, use_global_device_ids=true, to_apply=%region_8.9 | all-reduce | flops 1 | bytes 8 | tf_op jit(solution)/shard_map/psum | solution.py:11
  151.6 8.4 %all-gather.2 = f32[8,1,128]{2,1,0:T(1,128)S(1)} all-gather(f32[1,1,128]{2,1,0:T(1,128)S(1)} %bitcast.67), channel_id=1, replica_groups=mesh['group'=2,'row'=4,'col'=2,'sub'=2] {'row','sub'}, dimensions={0}, use_global_device_ids=true | all-gather | bytes 4608 | tf_op jit(solution)/shard_map/all_gather | solution.py:54
  160.0 1.2 fusion.10
  161.2 5.9 %all-reduce.1 = f32[512]{0:T(512)S(1)} all-reduce(f32[512]{0:T(512)S(1)} %bitcast.65), channel_id=4, replica_groups=mesh['group'=2,'row'=4,'col'=2,'sub'=2] {'col','sub'}, use_global_device_ids=true, to_apply=%region_9.10.clone | all-reduce | flops 512 | bytes 4096
  167.1 0.7 multiply_reduce_fusion
  167.8 31.1 %psum.31 = f32[]{:T(128)} all-reduce(f32[]{:T(128)} %multiply_reduce_fusion), channel_id=1, replica_groups=mesh['group'=2,'row'=4,'col'=2,'sub'=2] {'row','col','sub'}, use_global_device_ids=true, to_apply=%region_11.12 | all-reduce | flops 1 | bytes 8 | tf_op jit(solution)/shard_map/psum | solution.py:61
  200.2 0.6 multiply_subtract_fusion
  (10 shorter events, 0.1 us)
Async XLA Ops:
  7.2 23.6 %copy-start.3 = (u32[32]{0:T(128)S(1)}, u32[32]{0:T(128)}, u32[]{:S(2)}) copy-start(u32[32]{0:T(128)} %constant.61) | copy-start | bytes 388
  7.2 23.5 %copy-start = (f32[2048]{0:T(1024)S(1)}, f32[2048]{0:T(1024)}, u32[]{:S(2)}) copy-start(f32[2048]{0:T(1024)} %param.10) | copy-start | bytes 24580
  7.2 24.9 %copy-start.1 = (f32[128]{0:T(128)S(1)}, f32[128]{0:T(128)}, u32[]{:S(2)}) copy-start(f32[128]{0:T(128)} %param.8) | copy-start | bytes 1540
  9.1 20.8 %all-to-all-start = ((bf16[128,4,512]{2,0,1:T(8,128)(2,1)}), bf16[128,4,512]{2,0,1:T(8,128)(2,1)S(1)}, u32[]{:S(2)}, u32[]{:S(2)}) async-start(bf16[128,4,512]{2,0,1:T(8,128)(2,1)} %bitcast.41), calls=%async_computation | async-start | bytes 1048576 | tf_op jit(solution)/shard_map/all_to_all | solution.py:32
  15.4 42.4 %all-gather.5.cloned.1.call-start = ((), (), s32[]{:S(2)}) async-start(), calls=%async_computation.1 | async-start | bytes 1310720 | tf_op jit(solution)/shard_map/all_gather | solution.py:46
  78.2 7.6 %copy-start.2 = (f32[128]{0:T(128)S(1)}, f32[128]{0:T(128)}, u32[]{:S(2)}) copy-start(f32[128]{0:T(128)} %param.9) | copy-start | bytes 1540
Sparse Core Ops, SparseCore 0:
  30.8 27.0 all-gather.4
where the time goes:
time: 208 us
  blocking collectives  123 us (59%)
  waiting for transfers between devices  29.8 us (14%)
  between operations  18.8 us (9%)
  matrix products  10.1 us (5%)
  local copies, waits for them, and re-layouts  8.07 us (4%)
  loops' own time  7.89 us (4%)
  starting transfers between devices  6.32 us (3%)
  other arithmetic  3.32 us (2%)
    psum x2, blocking collectives, squares(): return lax.psum(jnp.sum(residual * residual), ('row', 'col', 'sub'))  61.7 us
    psum x1, blocking collectives, per_device(): lax.psum(jnp.sum(direction_vec * image), ('row', 'col', 'sub'))  31.1 us
    all_gather x2, blocking collectives, per_device(): lax.all_gather(direction_vec, ('row', 'sub'), axis=0, tiled=True)  18.2 us
    all_gather x1, waiting for transfers between devices, per_device(): piece = lax.all_gather(own_quarter[None], 'row', axis=0, tiled=True)  15.3 us
    all_to_all x1, waiting for transfers between devices, per_device(): lax.all_to_all(anomalies, 'row', split_axis=1, concat_axis=0, tiled=True)  14.5 us
    unnamed x2, blocking collectives  12.3 us
    another operation x1, loops' own time, per_device(): tiles = lax.map(one_entry, (piece, indices))  7.89 us
    dot_general x4, matrix products, one_tile(): jnp.einsum('mi,mq->iq', own_block, piece, preferred_element_type=jnp.floa...  7.74 us
  transfers between devices with their start and end apart: 2, of which 2 were waited for; matrix products, arithmetic and copies ran while one was open for 1% of the time, Pallas kernels for 0%

commit v1 on v0

--- a/solution.py
+++ b/solution.py
@@ -12,6 +12,19 @@
 
 
 def per_device(anomalies, innovations, obs_error, track_pos, taper_class):
+
+    def treat_matrix(inp, axis_tag):
+        cores_n = lax.axis_size(axis_tag)
+        o_now = [None] * cores_n
+        o_now[cores_n - 1] = inp
+        row_list = [(i, (i + 1) % cores_n) for i in range(cores_n)]
+        for hop_no in range(cores_n - 2, -1, -1):
+            o_now[hop_no] = lax.ppermute(o_now[hop_no + 1], axis_tag, perm=row_list)
+        a_next = jnp.concatenate(o_now, axis=0)
+        value_now = (lax.axis_index(axis_tag) + 1) * inp.shape[0]
+        base_arr = jnp.roll(a_next, value_now, axis=0)
+        return base_arr
+
     row_count = lax.axis_size("row")
     col_count = lax.axis_size("col")
     sub_count = lax.axis_size("sub")
@@ -43,7 +56,7 @@
     def one_entry(entry):
         return one_tile(entry[0], entry[1], 1.0)
 
-    piece = lax.all_gather(own_quarter[None], "row", axis=0, tiled=True)
+    piece = treat_matrix(own_quarter[None], "row")
     indices = jnp.arange(piece.shape[0], dtype=jnp.int32)
     tiles = lax.map(one_entry, (piece, indices))
     solution = jnp.zeros_like(innovations)

time: 208 us -> 199 us (0.957)
  between operations: 18.8 us -> 5.46 us
    ppermute x0 -> x3, waiting for transfers between devices: none -> 17.2 us  [treat_matrix(): o_now[hop_no] = lax.ppermute(o_now[hop_no + 1], axis_tag, perm=row_list)]
    all_gather x1 -> x0, waiting for transfers between devices: 15.3 us -> none  [per_device(): piece = lax.all_gather(own_quarter[None], 'row', axis=0, tiled=True)]
    all_gather x2, blocking collectives: 18.2 us -> 20.5 us  [per_device(): lax.all_gather(direction_vec, ('row', 'sub'), axis=0, tiled=True)]
  transfers between devices with their start and end apart: 2 -> 4, of which waited for: 2 -> 3; matrix products, arithmetic and copies ran while one was open for 1% -> 1% of each run, Pallas kernels for 0% -> 0%
where the time goes in v1:
time: 199 us; the launch traced here: 198 us
  blocking collectives  125 us (63%)
  waiting for transfers between devices  31.7 us (16%)
  matrix products  10.1 us (5%)
  local copies, waits for them, and re-layouts  8.57 us (4%)
  loops' own time  7.89 us (4%)
  starting transfers between devices  6.38 us (3%)
  between operations  5.46 us (3%)
  other arithmetic  3.32 us (2%)
    psum x2, blocking collectives, squares(): return lax.psum(jnp.sum(residual * residual), ('row', 'col', 'sub'))  60.2 us
    psum x1, blocking collectives, per_device(): lax.psum(jnp.sum(direction_vec * image), ('row', 'col', 'sub'))  31.1 us
    all_gather x2, blocking collectives, per_device(): lax.all_gather(direction_vec, ('row', 'sub'), axis=0, tiled=True)  20.5 us
    ppermute x3, waiting for transfers between devices, treat_matrix(): o_now[hop_no] = lax.ppermute(o_now[hop_no + 1], axis_tag, perm=row_list)  17.2 us
    all_to_all x1, waiting for transfers between devices, per_device(): lax.all_to_all(anomalies, 'row', split_axis=1, concat_axis=0, tiled=True)  14.5 us
    unnamed x2, blocking collectives  13 us
    another operation x1, loops' own time, per_device(): tiles = lax.map(one_entry, (piece, indices))  7.89 us
    dot_general x4, matrix products, one_tile(): jnp.einsum('mi,mq->iq', own_block, piece, preferred_element_type=jnp.floa...  7.75 us
  transfers between devices with their start and end apart: 4, of which 3 were waited for; matrix products, arithmetic and copies ran while one was open for 1% of the time, Pallas kernels for 0%

profile of v1, /device:TPU:0, one launch (start us, length us, event | category | flops | bytes accessed | tf_op | source)
XLA Modules:
  0.0 198.3 jit_solution(7910213217760824774)
XLA Ops:
  0.6 0.0 copy-start.3
  0.6 0.0 copy-start
  0.7 0.0 copy-start.1
  0.7 1.9 copy.16
  2.5 6.3 %all-to-all-start = ((bf16[128,4,512]{2,0,1:T(8,128)(2,1)}), bf16[128,4,512]{2,0,1:T(8,128)(2,1)S(1)}, u32[]{:S(2)}, u32[]{:S(2)}) async-start(bf16[128,4,512]{2,0,1:T(8,128)(2,1)} %bitcast.46), calls=%async_computation | async-start | bytes 1048576 | tf_op jit(solution)/shard_map/all_to_all | solution.py:45
  8.9 14.5 %all-to-all-done = bf16[128,4,512]{2,0,1:T(8,128)(2,1)S(1)} async-done(((bf16[128,4,512]{2,0,1:T(8,128)(2,1)}), bf16[128,4,512]{2,0,1:T(8,128)(2,1)S(1)}, u32[]{:S(2)}, u32[]{:S(2)}) %all-to-all-start) | async-done | bytes 524320 | tf_op jit(solution)/shard_map/all_to_all | solution.py:45
  23.4 0.1 collective-permute-start
  23.4 9.1 %collective-permute-done = bf16[1,512,256]{2,1,0:T(8,128)(2,1)S(1)} collective-permute-done((bf16[1,512,256]{2,1,0:T(8,128)(2,1)S(1)}, bf16[1,512,256]{2,1,0:T(8,128)(2,1)S(1)}, u32[]{:S(2)}, u32[]{:S(2)}) %collective-permute-start) | collective-permute-done | bytes 262176 | tf_op jit(solution)/shard_map/ppermute | solution.py:22
  32.5 0.0 collective-permute-start.1
  32.5 8.2 %collective-permute-done.1 = bf16[1,512,256]{2,1,0:T(8,128)(2,1)S(1)} collective-permute-done((bf16[1,512,256]{2,1,0:T(8,128)(2,1)S(1)}, bf16[1,512,256]{2,1,0:T(8,128)(2,1)S(1)}, u32[]{:S(2)}, u32[]{:S(2)}) %collective-permute-start.1) | collective-permute-done | bytes 262176 | tf_op jit(solution)/shard_map/ppermute | solution.py:22
  40.7 0.0 collective-permute-start.2
  40.7 0.0 copy-done
  40.7 0.1 dynamic_slice.37
  40.8 0.0 copy-done.3
  40.8 0.6 dynamic-slice
  42.0 0.0 copy-done.1
  42.1 12.2 %all-gather = f32[8,1,128]{2,1,0:T(1,128)S(1)} all-gather(f32[1,1,128]{2,1,0:T(1,128)S(1)} %bitcast.71), channel_id=1, replica_groups=mesh['group'=2,'row'=4,'col'=2,'sub'=2] {'row','sub'}, dimensions={0}, use_global_device_ids=true | all-gather | bytes 4608 | tf_op jit(solution)/shard_map/all_gather | solution.py:67
  54.2 0.7 maximum_bitcast_fusion
  54.9 0.0 collective-permute-done.2
  55.1 1.1 constant_dynamic-slice_fusion.3
  56.2 20.4 %while.10 = (s32[]{:T(128)}, f32[4,512,256]{1,2,0:T(8,128)S(1)}, bf16[4,512,256]{2,1,0:T(8,128)(2,1)}, bf16[512,512]{1,0:T(8,128)(2,1)S(1)}, s32[4]{0:T(128)S(1)...) while((s32[]{:T(128)}, f32[4,512,256]{1,2,0:T(8,128)S(1)}, ...), condition=%wide.region_3.4_spmd, body=%wide.region_2.3_spmd.sunk | while | flops 135135232 | bytes 1317547 | solution.py:61
  56.2 0.6 dynamic_slice.66
  58.7 0.6 dynamic_slice.67
  59.3 1.9 fusion.21
  61.3 0.6 dynamic_slice.66
  63.8 0.6 dynamic_slice.67
  64.4 1.9 fusion.21
  66.4 0.6 dynamic_slice.66
  68.9 0.6 dynamic_slice.67
  69.5 1.9 fusion.21
  71.5 0.6 dynamic_slice.66
  74.0 0.6 dynamic_slice.67
  74.6 1.9 fusion.21
  76.6 0.0 copy-start.2
  76.6 1.2 fusion.9
  77.8 7.0 %all-reduce = f32[512]{0:T(512)S(1)} all-reduce(f32[512]{0:T(512)S(1)} %bitcast.73), channel_id=2, replica_groups=mesh['group'=2,'row'=4,'col'=2,'sub'=2] {'col','sub'}, use_global_device_ids=true, to_apply=%region_4.5.clone | all-reduce | flops 512 | bytes 4096
  84.8 0.0 copy-done.2
  84.8 0.7 multiply_reduce_fusion.2
  85.5 30.1 %all-reduce.2 = (f32[]{:T(128)}, f32[]{:T(128)}) all-reduce(f32[]{:T(128)} %get-tuple-element.46, f32[]{:T(128)} %get-tuple-element.45), channel_id=1, replica_groups=mesh['group'=2,'row'=4,'col'=2,'sub'=2] {'row','col','sub'}, use_global_device_ids=true, to_apply=%region_1.2 | all-reduce | flops 2 | bytes 16 | tf_op jit(solution)/shard_map/psum | solution.py:11
  116.9 0.7 multiply_reduce_fusion.1
  117.6 30.1 %psum.30 = f32[]{:T(128)} all-reduce(f32[]{:T(128)} %get-tuple-element.65), channel_id=1, replica_groups=mesh['group'=2,'row'=4,'col'=2,'sub'=2] {'row','col','sub'}, use_global_device_ids=true, to_apply=%region_8.9 | all-reduce | flops 1 | bytes 8 | tf_op jit(solution)/shard_map/psum | solution.py:11
  149.1 8.4 %all-gather.1 = f32[8,1,128]{2,1,0:T(1,128)S(1)} all-gather(f32[1,1,128]{2,1,0:T(1,128)S(1)} %bitcast.74), channel_id=1, replica_groups=mesh['group'=2,'row'=4,'col'=2,'sub'=2] {'row','sub'}, dimensions={0}, use_global_device_ids=true | all-gather | bytes 4608 | tf_op jit(solution)/shard_map/all_gather | solution.py:67
  157.4 1.2 fusion.10
  158.6 5.9 %all-reduce.1 = f32[512]{0:T(512)S(1)} all-reduce(f32[512]{0:T(512)S(1)} %bitcast.72), channel_id=3, replica_groups=mesh['group'=2,'row'=4,'col'=2,'sub'=2] {'col','sub'}, use_global_device_ids=true, to_apply=%region_9.10.clone | all-reduce | flops 512 | bytes 4096
  164.6 0.7 multiply_reduce_fusion
  165.2 31.1 %psum.31 = f32[]{:T(128)} all-reduce(f32[]{:T(128)} %multiply_reduce_fusion), channel_id=1, replica_groups=mesh['group'=2,'row'=4,'col'=2,'sub'=2] {'row','col','sub'}, use_global_device_ids=true, to_apply=%region_11.12 | all-reduce | flops 1 | bytes 8 | tf_op jit(solution)/shard_map/psum | solution.py:74
  197.7 0.6 multiply_subtract_fusion
  (19 shorter events, 0.2 us)
Async XLA Ops:
  0.6 40.2 %copy-start.3 = (u32[32]{0:T(128)S(1)}, u32[32]{0:T(128)}, u32[]{:S(2)}) copy-start(u32[32]{0:T(128)} %constant.83) | copy-start | bytes 388
  0.6 40.0 %copy-start = (f32[2048]{0:T(1024)S(1)}, f32[2048]{0:T(1024)}, u32[]{:S(2)}) copy-start(f32[2048]{0:T(1024)} %param.10) | copy-start | bytes 24580
  0.7 41.4 %copy-start.1 = (f32[128]{0:T(128)S(1)}, f32[128]{0:T(128)}, u32[]{:S(2)}) copy-start(f32[128]{0:T(128)} %param.8) | copy-start | bytes 1540
  2.5 20.8 %all-to-all-start = ((bf16[128,4,512]{2,0,1:T(8,128)(2,1)}), bf16[128,4,512]{2,0,1:T(8,128)(2,1)S(1)}, u32[]{:S(2)}, u32[]{:S(2)}) async-start(bf16[128,4,512]{2,0,1:T(8,128)(2,1)} %bitcast.46), calls=%async_computation | async-start | bytes 1048576 | tf_op jit(solution)/shard_map/all_to_all | solution.py:45
  23.4 9.1 %collective-permute-start = (bf16[1,512,256]{2,1,0:T(8,128)(2,1)S(1)}, bf16[1,512,256]{2,1,0:T(8,128)(2,1)S(1)}, u32[]{:S(2)}, u32[]{:S(2)}) collective-permute-start(bf16[1,512,256]{2,1,0:T(8,128)(2,1)S(1)} %dynamic-slice_bitcast_fusion), channel_id=1, source_target_pairs={{0,4},{4,8},{8,12},{12,0},{1,5},{5,9},{9,13},{13,1},{2,6},{6,10},{... | collective-permute-start | bytes 786440 | tf_op jit(solution)/shard_map/ppermute | solution.py:22
  32.5 8.2 %collective-permute-start.1 = (bf16[1,512,256]{2,1,0:T(8,128)(2,1)S(1)}, bf16[1,512,256]{2,1,0:T(8,128)(2,1)S(1)}, u32[]{:S(2)}, u32[]{:S(2)}) collective-permute-start(bf16[1,512,256]{2,1,0:T(8,128)(2,1)S(1)} %collective-permute-done), channel_id=1, source_target_pairs={{0,4},{4,8},{8,12},{12,0},{1,5},{5,9},{9,13},{13,1},{2,6},{6,10},{... | collective-permute-start | bytes 786440 | tf_op jit(solution)/shard_map/ppermute | solution.py:22
  40.7 14.2 %collective-permute-start.2 = (bf16[1,512,256]{2,1,0:T(8,128)(2,1)S(1)}, bf16[1,512,256]{2,1,0:T(8,128)(2,1)S(1)}, u32[]{:S(2)}, u32[]{:S(2)}) collective-permute-start(bf16[1,512,256]{2,1,0:T(8,128)(2,1)S(1)} %collective-permute-done.1), channel_id=1, source_target_pairs={{0,4},{4,8},{8,12},{12,0},{1,5},{5,9},{9,13},{13,1},{2,6},{6,10},{... | collective-permute-start | bytes 786440 | tf_op jit(solution)/shard_map/ppermute | solution.py:22
  76.6 8.2 %copy-start.2 = (f32[128]{0:T(128)S(1)}, f32[128]{0:T(128)}, u32[]{:S(2)}) copy-start(f32[128]{0:T(128)} %param.9) | copy-start | bytes 1540
